TPU v7x, 32 devices: a whole 2x2x4 slice. The times are simulated.
32 devices in a mesh: win: 8 (over y, x, core), seq: 4 (over z).
Axes of the slice: x: 2, y: 2, z: 4, core: 2. Of those that a mesh axis runs over, the one named last changes fastest.
Arguments:
- qkv_grid: bfloat16 [90, 8, 32, 4608], P(None, 'win', 'seq'), may hold values from -160 to 160
- tokens: bfloat16 [90, 8, 32, 1536], P(None, 'win', 'seq'), may hold values from -6 to 6
- out_weight: bfloat16 [1536, 1536], replicated, may hold values from -0.625 to 0.625
- regions: int32 [90, 8, 32], P(None, 'win'), may hold values from 0 to 2, as said below
Outputs:
- mixed: bfloat16 [90, 8, 32, 1536], P(None, 'win', 'seq')
Inputs may be any that keep to these rules, and one draw needn't show every extreme that they name: `regions`: columns 2m and 2m+1 of a window always have the same region id.
All inputs are finite; a program needn't handle non-finite values.
Results may differ from a plain program's by a relative error of at most 0.01.
Values may be sent and summed in bfloat16 or wider, within the bound.
A program may use at most 128 MiB of HBM per device.

v0:
```python
import jax
import jax.numpy as jnp
from jax import lax
from jax.sharding import PartitionSpec as P

D = 1536
HEADS = 16
HD = 96
WH = 30
WW = 32


def from_behind(block, axis, distance):
    devices = range(lax.axis_size(axis))
    route = [((i - distance) % len(devices), i) for i in devices]
    return lax.ppermute(block, axis, route)


def attend(window_block, labels):
    queries = window_block[:, 0]
    key_rows = window_block[:, 1]
    values = window_block[:, 2]
    scores = jnp.einsum(
        "qhd,khd->hqk", queries, key_rows, preferred_element_type=jnp.float32
    ) * HD ** (-0.5)
    allowed = labels[:, None] == labels[None, :]
    scores = jnp.where(allowed[None], scores, -1e30)
    largest = jnp.max(scores, axis=-1, keepdims=True)
    weights = jnp.exp(scores - largest)
    soft_weights = (weights / jnp.sum(weights, axis=-1, keepdims=True)).astype(jnp.bfloat16)
    result = jnp.einsum("hqk,khd->qhd", soft_weights, values, preferred_element_type=jnp.float32)
    return result.astype(jnp.bfloat16)


def one_window(paired):
    return attend(paired[0], paired[1])


def window_attention(flat_grid, labels_flat):
    row_total, col_total, three, heads_here, head_size = flat_grid.shape
    bands = row_total // WH
    window_count = col_total // WW
    blocks = flat_grid.reshape(bands, WH, window_count, WW, three, heads_here, head_size)
    blocks = blocks.transpose(0, 2, 1, 3, 4, 5, 6).reshape(
        bands * window_count, WH * WW, three, heads_here, head_size
    )
    labels = (
        labels_flat.reshape(bands, WH, window_count, WW)
        .transpose(0, 2, 1, 3)
        .reshape(bands * window_count, WH * WW)
    )
    attended = lax.map(one_window, (blocks, labels))
    attended = attended.reshape(bands, window_count, WH, WW, heads_here, head_size).transpose(
        0, 2, 1, 3, 4, 5
    )
    return attended.reshape(row_total, col_total, heads_here, head_size)


def per_device(qkv_grid, tokens, out_weight, regions):
    seq_count = lax.axis_size("seq")
    lat_rows, win_count, col_count, packed_width = qkv_grid.shape
    labels_local = regions.reshape(lat_rows, win_count * WW)
    half_cols = WW // 2
    half_rows = WH // 2
    group_heads = HEADS // seq_count
    split_heads = qkv_grid.reshape(lat_rows, win_count, col_count, 3, seq_count, group_heads, HD)
    gathered = lax.all_to_all(split_heads, "seq", split_axis=4, concat_axis=2, tiled=True)
    flat_grid = gathered.reshape(lat_rows, win_count * WW, 3, group_heads, HD)
    arriving = from_behind(flat_grid[:, :half_cols], "win", -1)
    shifted = jnp.concatenate([flat_grid[:, half_cols:], arriving], axis=1)
    shifted = jnp.roll(shifted, -half_rows, axis=0)
    result = window_attention(shifted, labels_local)
    result = jnp.roll(result, half_rows, axis=0)
    leaving = from_behind(result[:, -half_cols:], "win", 1)
    result = jnp.concatenate([leaving, result[:, :-half_cols]], axis=1)
    attended = result.reshape(lat_rows, win_count, WW, 1, group_heads, HD)
    returned = lax.all_to_all(attended, "seq", split_axis=2, concat_axis=3, tiled=True)
    mixed_in = returned.reshape(lat_rows, win_count, col_count, D)
    projected = jnp.dot(mixed_in.reshape(-1, D), out_weight, preferred_element_type=jnp.float32)
    total = projected + tokens.reshape(-1, D).astype(jnp.float32)
    return total.astype(jnp.bfloat16).reshape(tokens.shape)


def solution(mesh):
    in_specs = (P(None, "win", "seq", None), P(None, "win", "seq", None), P(), P(None, "win", None))
    out_specs = P(None, "win", "seq", None)
    return jax.shard_map(
        per_device, mesh=mesh, in_specs=in_specs, out_specs=out_specs, check_vma=False
    )
```

profile of v0, /device:TPU:8, one launch (start us, length us, event | category | flops | bytes accessed | tf_op | source)
XLA Modules:
  0.0 487.5 jit_solution(6502701629563649295)
XLA Ops:
  0.0 17.0 %reshape.50 = bf16[90,1,8,3,4,4,96]{6,5,4,3,2,0,1:T(4,128)(2,1)} reshape(bf16[90,1,8,4608]{3,2,1,0:T(8,128)(2,1)} %param.6) | data formatting | bytes 13271040 | tf_op jit(solution)/shard_map/reshape | solution.py:66
  17.0 5.5 %copy.34 = bf16[90,1,8,3,4,4,96]{6,5,3,2,0,1,4:T(4,128)(2,1)S(1)} copy(bf16[90,1,8,3,4,4,96]{6,5,4,3,2,0,1:T(4,128)(2,1)} %reshape.50) | data formatting | bytes 13271040 | tf_op jit(solution)/shard_map/reshape | solution.py:66
  22.6 196.4 %all_to_all.30 = bf16[90,1,8,3,4,4,96]{6,5,3,2,0,1,4:T(4,128)(2,1)} all-to-all(bf16[90,1,8,3,4,4,96]{6,5,3,2,0,1,4:T(4,128)(2,1)S(1)} %copy.34), channel_id=1, replica_groups=mesh['win'=8,'seq'=4] {'seq'}, dimensions={4} | all-to-all | bytes 13271040 | tf_op jit(solution)/shard_map/all_to_all | solution.py:67
  219.0 9.7 %copy.46 = bf16[90,1,8,3,4,4,96]{6,2,4,5,3,0,1:T(8,128)(2,1)} copy(bf16[90,1,8,3,4,4,96]{6,5,3,2,0,1,4:T(4,128)(2,1)} %all_to_all.30) | data formatting | bytes 13271040 | tf_op jit(solution)/shard_map/all_to_all | solution.py:67
  228.7 9.3 %fusion.22 = (bf16[90,16,3,4,96]{4,1,3,2,0:T(8,128)(2,1)}, bf16[90,16,3,4,96]{4,1,3,2,0:T(8,128)(2,1)}) fusion(bf16[90,32,3,4,96]{4,1,3,2,0:T(8,128)(2,1)} %bitcast.76), kind=kLoop, calls=%fused_computation.39 | loop fusion | bytes 13271040 | tf_op jit(solution)/shard_map/slice | solution.py:70
  238.0 0.6 collective-permute-start
  238.9 48.6 %collective-permute-done = bf16[90,16,3,4,96]{4,1,3,2,0:T(8,128)(2,1)} collective-permute-done((bf16[90,16,3,4,96]{4,1,3,2,0:T(8,128)(2,1)}, bf16[90,16,3,4,96]{4,1,3,2,0:T(8,128)(2,1)}, u32[]{:S(2)}, u32[]{:S(2)}) %collective-permute-start) | collective-permute-done | bytes 3317792 | tf_op jit(solution)/shard_map/ppermute | solution.py:16
  287.5 5.2 %fusion.15 = bf16[75,32,3,4,96]{4,1,3,2,0:T(8,128)(2,1)S(1)} fusion(bf16[90,16,3,4,96]{4,1,3,2,0:T(8,128)(2,1)} %get-tuple-element.54, bf16[90,16,3,4,96]{4,1,3,2,0:T(8,128)(2,1)} %collective-permute-done), kind=kLoop, calls=%fused_computation.27 | loop fusion | flops 11059200 | bytes 12165120 | tf_op jit(solution)/shard_map/concatenate | solution.py:70
  292.7 6.0 %fusion.14 = bf16[90,32,3,4,96]{4,1,3,2,0:T(8,128)(2,1)} fusion(bf16[90,16,3,4,96]{4,1,3,2,0:T(8,128)(2,1)} %collective-permute-done, bf16[90,16,3,4,96]{4,1,3,2,0:T(8,128)(2,1)S(1)} %copy-done, bf16[75,32,3,4,96]{4,1,3,2,0:T(8,128)(2,1)S(1)} %fusion.15), kind=kLoop, calls=%fused_computation.23 | loop fusion | flops 19906560 | bytes 18800640 | tf_op jit(solution)/shard_map/jit(_roll_static)/concatenate | solution.py:71
  298.6 9.0 %copy.36 = bf16[90,32,3,4,96]{4,1,0,3,2:T(8,128)(2,1)} copy(bf16[90,32,3,4,96]{4,1,3,2,0:T(8,128)(2,1)} %fusion.14) | data formatting | bytes 13271040 | tf_op jit(solution)/shard_map/jit(_roll_static)/concatenate | solution.py:71
  307.6 11.3 %copy.38 = bf16[3,960,3,4,96]{1,4,3,2,0:T(8,128)(2,1)} copy(bf16[3,960,3,4,96]{4,1,0,3,2:T(8,128)(2,1)} %bitcast.77) | data formatting | bytes 13271040 | tf_op jit(solution)/shard_map/while | solution.py:52
  318.8 59.7 %while.10 = (s32[]{:T(128)}, bf16[3,960,4,96]{1,3,2,0:T(8,128)(2,1)}, bf16[3,960,3,4,96]{1,4,3,2,0:T(8,128)(2,1)}, s32[3,960]{1,0:T(4,128)S(1)}, s32[]{:T(128)}) while((s32[]{:T(128)}, bf16[3,960,4,96]{1,3,2,0:T(8,128)(2,1)}, bf16[3,960,3,4,96]{1,4,3,2,0:T(8,128)(2,1)}, s32[3,960]{1,0:T(4,128)S(1)}, s32[]{:T(128)}) %tuple.26), condition=%wide.region_3.4_spmd, body=%wide.region_0.3_spmd.sunk | while | flops 1438987264 | bytes 39992132 | solution.py:52
  318.8 2.0 dynamic-slice_bitcast_fusion.2
  320.9 0.6 broadcast_compare_fusion.2
  321.5 9.5 %fusion.27 = (f32[4,960]{1,0:T(4,128)S(1)}, f32[4,960,960]{1,2,0:T(8,128)}) fusion(pred[960,960]{0,1:T(8,128)(4,1)S(1)} %broadcast_compare_fusion.2, bf16[960,3,4,96]{0,3,2,1:T(8,128)(2,1)S(1)} %dynamic-slice_bitcast_fusion.2), kind=kOutput, calls=%fused_computation.38.clone.1 | convolution fusion | flops 722535360 | bytes 17316864 | tf_op jit(solution)/shard_map/while/body/eval_jaxpr/sub | solution.py:29
  331.0 7.7 %fusion.28 = bf16[3,960,4,96]{1,3,2,0:T(8,128)(2,1)} fusion(bf16[3,960,4,96]{1,3,2,0:T(8,128)(2,1)} %get-tuple-element.91, s32[]{:T(128)} %get-tuple-element.90, f32[4,960,960]{1,2,0:T(8,128)} %get-tuple-element.83, f32[4,960]{1,0:T(4,128)S(1)} %get-tuple-element.84, bf16[960,3,4,96]{0,3,2,1:T(8,128)(2,1)S(1)} %dynamic-slice_bitcast_fusion.2), kind=kOutput, calls=%fused_computation.14.clone.1 | convolution fusion | flops 715530240 | bytes 17318400 | tf_op jit(solution)/shard_map/while/body/eval_jaxpr/hqk,khd->qhd/dot_general | solution.py:31
  338.7 2.0 dynamic-slice_bitcast_fusion.2
  340.8 0.6 broadcast_compare_fusion.2
  341.4 9.5 %fusion.27 = (f32[4,960]{1,0:T(4,128)S(1)}, f32[4,960,960]{1,2,0:T(8,128)}) fusion(pred[960,960]{0,1:T(8,128)(4,1)S(1)} %broadcast_compare_fusion.2, bf16[960,3,4,96]{0,3,2,1:T(8,128)(2,1)S(1)} %dynamic-slice_bitcast_fusion.2), kind=kOutput, calls=%fused_computation.38.clone.1 | convolution fusion | flops 722535360 | bytes 17316864 | tf_op jit(solution)/shard_map/while/body/eval_jaxpr/sub | solution.py:29
  350.9 7.8 %fusion.28 = bf16[3,960,4,96]{1,3,2,0:T(8,128)(2,1)} fusion(bf16[3,960,4,96]{1,3,2,0:T(8,128)(2,1)} %get-tuple-element.91, s32[]{:T(128)} %get-tuple-element.90, f32[4,960,960]{1,2,0:T(8,128)} %get-tuple-element.83, f32[4,960]{1,0:T(4,128)S(1)} %get-tuple-element.84, bf16[960,3,4,96]{0,3,2,1:T(8,128)(2,1)S(1)} %dynamic-slice_bitcast_fusion.2), kind=kOutput, calls=%fused_computation.14.clone.1 | convolution fusion | flops 715530240 | bytes 17318400 | tf_op jit(solution)/shard_map/while/body/eval_jaxpr/hqk,khd->qhd/dot_general | solution.py:31
  358.6 2.0 dynamic-slice_bitcast_fusion.2
  360.7 0.6 broadcast_compare_fusion.2
  361.3 9.5 %fusion.27 = (f32[4,960]{1,0:T(4,128)S(1)}, f32[4,960,960]{1,2,0:T(8,128)}) fusion(pred[960,960]{0,1:T(8,128)(4,1)S(1)} %broadcast_compare_fusion.2, bf16[960,3,4,96]{0,3,2,1:T(8,128)(2,1)S(1)} %dynamic-slice_bitcast_fusion.2), kind=kOutput, calls=%fused_computation.38.clone.1 | convolution fusion | flops 722535360 | bytes 17316864 | tf_op jit(solution)/shard_map/while/body/eval_jaxpr/sub | solution.py:29
  370.8 7.8 %fusion.28 = bf16[3,960,4,96]{1,3,2,0:T(8,128)(2,1)} fusion(bf16[3,960,4,96]{1,3,2,0:T(8,128)(2,1)} %get-tuple-element.91, s32[]{:T(128)} %get-tuple-element.90, f32[4,960,960]{1,2,0:T(8,128)} %get-tuple-element.83, f32[4,960]{1,0:T(4,128)S(1)} %get-tuple-element.84, bf16[960,3,4,96]{0,3,2,1:T(8,128)(2,1)S(1)} %dynamic-slice_bitcast_fusion.2), kind=kOutput, calls=%fused_computation.14.clone.1 | convolution fusion | flops 715530240 | bytes 17318400 | tf_op jit(solution)/shard_map/while/body/eval_jaxpr/hqk,khd->qhd/dot_general | solution.py:31
  378.5 3.3 copy.39
  382.6 1.4 collective-permute-start.1
  384.0 18.7 %collective-permute-done.1 = bf16[90,16,4,96]{3,1,0,2:T(8,128)(2,1)S(1)} collective-permute-done((bf16[90,16,4,96]{3,1,0,2:T(8,128)(2,1)S(1)}, bf16[90,16,4,96]{3,1,0,2:T(8,128)(2,1)S(1)}, u32[]{:S(2)}, u32[]{:S(2)}) %collective-permute-start.1) | collective-permute-done | bytes 1105952 | tf_op jit(solution)/shard_map/ppermute | solution.py:16
  403.3 2.3 copy.40
  405.6 67.3 %all_to_all.31 = bf16[90,1,32,1,4,96]{5,4,3,1,0,2:T(4,128)(2,1)S(1)} all-to-all(bf16[90,1,32,1,4,96]{5,4,3,1,0,2:T(4,128)(2,1)S(1)} %copy.40), channel_id=1, replica_groups=mesh['win'=8,'seq'=4] {'seq'}, dimensions={2} | all-to-all | bytes 4423680 | tf_op jit(solution)/shard_map/all_to_all | solution.py:77
  472.9 1.6 copy.47
  474.6 4.3 reshape_reshape.3
  478.9 8.6 %fusion.19 = bf16[90,1,8,1536]{3,2,1,0:T(8,128)(2,1)} fusion(bf16[720,1536]{1,0:T(8,128)(2,1)} %reshape_reshape.3, bf16[1536,1536]{1,0:T(8,128)(2,1)} %param.8, bf16[90,1,8,1536]{3,2,1,0:T(8,128)(2,1)} %param.7), kind=kOutput, calls=%fused_computation.36 | convolution fusion | flops 3400704000 | bytes 11354112 | tf_op jit(solution)/shard_map/dot_general | solution.py:79
  (14 shorter events, 1.5 us)
Async XLA Ops:
  228.7 10.0 %copy-start.1 = (s32[90,1,32]{0,2,1:T(8,128)S(1)}, s32[90,1,32]{0,2,1:T(8,128)}, u32[]{:S(2)}) copy-start(s32[90,1,32]{0,2,1:T(8,128)} %param.9) | copy-start | bytes 34564
  238.0 49.4 %collective-permute-start = (bf16[90,16,3,4,96]{4,1,3,2,0:T(8,128)(2,1)}, bf16[90,16,3,4,96]{4,1,3,2,0:T(8,128)(2,1)}, u32[]{:S(2)}, u32[]{:S(2)}) collective-permute-start(bf16[90,16,3,4,96]{4,1,3,2,0:T(8,128)(2,1)} %get-tuple-element.55), channel_id=1, source_target_pairs={{4,0},{8,4},{12,8},{16,12},{20,16},{24,20},{28,24},{0,28},{5,1},{9... | collective-permute-start | bytes 9953288 | tf_op jit(solution)/shard_map/ppermute | solution.py:16
  287.5 5.2 %copy-start = (bf16[90,16,3,4,96]{4,1,3,2,0:T(8,128)(2,1)S(1)}, bf16[90,16,3,4,96]{4,1,3,2,0:T(8,128)(2,1)}, u32[]{:S(2)}) copy-start(bf16[90,16,3,4,96]{4,1,3,2,0:T(8,128)(2,1)} %get-tuple-element.54) | copy-start | bytes 9953284
  382.6 20.1 %collective-permute-start.1 = (bf16[90,16,4,96]{3,1,0,2:T(8,128)(2,1)S(1)}, bf16[90,16,4,96]{3,1,0,2:T(8,128)(2,1)S(1)}, u32[]{:S(2)}, u32[]{:S(2)}) collective-permute-start(bf16[90,16,4,96]{3,1,0,2:T(8,128)(2,1)S(1)} %fusion.20), channel_id=1, source_target_pairs={{28,0},{0,4},{4,8},{8,12},{12,16},{16,20},{20,24},{24,28},{29,1},{... | collective-permute-start | bytes 3317768 | tf_op jit(solution)/shard_map/ppermute | solution.py:16
where the time goes:
time: 491 us; the launch traced here: 488 us
  blocking collectives  264 us (54%)
  local copies, waits for them, and re-layouts  80.1 us (16%)
  waiting for transfers between devices  67.3 us (14%)
  matrix products  60.3 us (12%)
  other arithmetic  13.8 us (3%)
    all_to_all x1, blocking collectives, per_device(): lax.all_to_all(split_heads, 'seq', split_axis=4, concat_axis=2, tiled=True)  196 us
    all_to_all x1, blocking collectives, per_device(): lax.all_to_all(attended, 'seq', split_axis=2, concat_axis=3, tiled=True)  67.3 us
    ppermute x2, waiting for transfers between devices, from_behind(): return lax.ppermute(block, axis, route)  67.3 us
    sub x3, matrix products, attend(): weights = jnp.exp(scores - largest)  28.4 us
    dot_general x3, matrix products, attend(): jnp.einsum('hqk,khd->qhd', soft_weights, values, preferred_element_type=j...  23.3 us
    reshape x2, local copies, waits for them, and re-layouts, per_device(): qkv_grid.reshape(lat_rows, win_count, col_count, 3, seq_count, group_head...  22.6 us
    while x2, local copies, waits for them, and re-layouts, window_attention(): attended = lax.map(one_window, (blocks, labels))  14.6 us
  transfers between devices with their start and end apart: 2, of which 2 were waited for; matrix products, arithmetic and copies ran while one was open for 0% of the time, Pallas kernels for 0%

commit v1 on v0

--- a/solution.py
+++ b/solution.py
@@ -1,6 +1,10 @@
+import functools
+
 import jax
 import jax.numpy as jnp
 from jax import lax
+from jax.experimental import pallas as pl
+from jax.experimental.pallas import tpu as pltpu
 from jax.sharding import PartitionSpec as P
 
 D = 1536
@@ -56,7 +60,7 @@
     return attended.reshape(row_total, col_total, heads_here, head_size)
 
 
-def per_device(qkv_grid, tokens, out_weight, regions):
+def general_device(qkv_grid, tokens, out_weight, regions):
     seq_count = lax.axis_size("seq")
     lat_rows, win_count, col_count, packed_width = qkv_grid.shape
     labels_local = regions.reshape(lat_rows, win_count * WW)
@@ -81,6 +85,344 @@
     return total.astype(jnp.bfloat16).reshape(tokens.shape)
 
 
+LANES = 128
+ROWS8 = 8
+FAR = -1e30
+LOG2E = 1.4426950408889634
+REGION_SLOTS = 3
+
+
+def head_span(head):
+    first = head * HD // LANES
+    last = ((head + 1) * HD - 1) // LANES
+    return first, last + 1, head * HD - first * LANES
+
+
+def spare_lane(head):
+    first, last, start = head_span(head)
+    return 0 if start > 0 else HD
+
+
+def fused_kernel(
+    windows,
+    members,
+    bands,
+    cols,
+    qkv_ref,
+    tokens_ref,
+    weight_ref,
+    label_ref,
+    out_ref,
+    arrived,
+    label_v,
+    weight_v,
+    token_v,
+    q_h,
+    k_h,
+    v_h,
+    result,
+    gathered,
+    out_v,
+    send_sem,
+    recv_sem,
+    own_sem,
+    back_send,
+    back_recv,
+    back_own,
+    token_sem,
+    out_sem,
+    misc_sem,
+):
+    half_rows = WH // 2
+    half_n = members // 2
+    group = D // members
+    heads = HEADS // members
+    block = WH * cols
+    lat = bands * WH
+    w = lax.axis_index("win")
+    s = lax.axis_index("seq")
+    low = 1 - s // half_n
+    home = lax.rem(w + windows - low, windows)
+    me = lax.rem(s + half_n, members)
+
+    def member_at(distance):
+        return lax.rem(me + distance, members)
+
+    def device_of(member):
+        seat = lax.rem(member + half_n, members)
+        column = lax.rem(home + 1 - seat // half_n, windows)
+        return {"win": column, "seq": seat}
+
+    def grid_row(band, part):
+        return lax.rem(half_rows * (2 * band + part + 1), lat)
+
+    def features(kind, member):
+        return pl.ds(pl.multiple_of(kind * D + member * group, LANES), group)
+
+    def outgoing(band, distance, kind, part):
+        target = member_at(distance)
+        return pltpu.make_async_remote_copy(
+            src_ref=qkv_ref.at[pl.ds(grid_row(band, part), half_rows), :, features(kind, target)],
+            dst_ref=arrived.at[band, kind, me, pl.ds(part * half_rows, half_rows)],
+            send_sem=send_sem.at[band, distance - 1, kind, part],
+            recv_sem=recv_sem.at[band, distance - 1, kind, part],
+            device_id=device_of(target),
+            device_id_type=pl.DeviceIdType.MESH,
+        )
+
+    def own(band, kind, part):
+        return pltpu.make_async_copy(
+            qkv_ref.at[pl.ds(grid_row(band, part), half_rows), :, features(kind, me)],
+            arrived.at[band, kind, me, pl.ds(part * half_rows, half_rows)],
+            own_sem.at[band, kind, part],
+        )
+
+    def token_copy(band, part):
+        return pltpu.make_async_copy(
+            tokens_ref.at[pl.ds(grid_row(band, part), half_rows)],
+            token_v.at[band, pl.ds(part * half_rows, half_rows)],
+            token_sem.at[band, part],
+        )
+
+    def out_copy(band, part):
+        return pltpu.make_async_copy(
+            out_v.at[band, pl.ds(part * half_rows, half_rows)],
+            out_ref.at[pl.ds(grid_row(band, part), half_rows)],
+            out_sem.at[band, part],
+        )
+
+    def rows_of(member):
+        return pl.ds(pl.multiple_of(member * block, block), block)
+
+    def homeward(band, distance):
+        target = member_at(distance)
+        return pltpu.make_async_remote_copy(
+            src_ref=result.at[band, rows_of(target)],
+            dst_ref=gathered.at[band, :, features(0, me)],
+            send_sem=back_send.at[band, distance - 1],
+            recv_sem=back_recv.at[band, distance - 1],
+            device_id=device_of(target),
+            device_id_type=pl.DeviceIdType.MESH,
+        )
+
+    def stay(band):
+        return pltpu.make_async_copy(
+            result.at[band, rows_of(me)],
+            gathered.at[band, :, features(0, me)],
+            back_own.at[band],
+        )
+
+    label_copy = pltpu.make_async_copy(label_ref, label_v, misc_sem.at[0])
+    weight_copy = pltpu.make_async_copy(weight_ref, weight_v, misc_sem.at[1])
+
+    barrier = pltpu.get_barrier_semaphore()
+    for distance in range(1, members):
+        pl.semaphore_signal(
+            barrier,
+            inc=1,
+            device_id=device_of(member_at(distance)),
+            device_id_type=pl.DeviceIdType.MESH,
+        )
+    pl.semaphore_wait(barrier, members - 1)
+
+    pieces = [(kind, part) for kind in range(3) for part in range(2)]
+
+    def launch(band, carry):
+        for kind, part in pieces:
+            for distance in range(1, members):
+                outgoing(band, distance, kind, part).start()
+        for kind, part in pieces:
+            own(band, kind, part).start()
+        return carry
+
+    lax.fori_loop(0, bands, launch, 0)
+    label_copy.start()
+    weight_copy.start()
+    for band in range(bands):
+        for part in range(2):
+            token_copy(band, part).start()
+    label_copy.wait()
+
+    lane = lax.broadcasted_iota(jnp.int32, (block, LANES), 1)
+    slot = lax.rem(lane, 32).astype(jnp.float32)
+
+    def prepare(band, member):
+        rows = rows_of(member)
+        label = label_v[band, rows, :].astype(jnp.float32)
+        same = slot == label
+        query_fill = jnp.where(same, FAR, 0.0)
+        key_fill = jnp.where(same, 0.0, jnp.where(slot < REGION_SLOTS, 1.0, 0.0))
+        ones = jnp.ones((block, LANES), jnp.float32)
+        for kind, target, fill in ((0, q_h, query_fill), (1, k_h, key_fill), (2, v_h, ones)):
+            wide = arrived[band, kind, member].astype(jnp.float32).reshape(block, group)
+            for head in range(heads):
+                first, last, start = head_span(head)
+                for tile in range(first, last):
+                    place = lane + (tile - first) * LANES
+                    inside = (place >= start) & (place < start + HD)
+                    chosen = jnp.where(inside, wide[:, tile * LANES : (tile + 1) * LANES], fill)
+                    spot = (tile - first) * LANES
+                    target[head, rows, spot : spot + LANES] = chosen.astype(jnp.bfloat16)
+
+    def attend_band(band, carry):
+        for kind, part in pieces:
+            own(band, kind, part).wait()
+            for distance in range(1, members):
+                outgoing(band, distance, kind, part).wait_recv()
+
+        def prepare_step(member, inner):
+            prepare(band, member)
+            return inner
+
+        lax.fori_loop(0, members, prepare_step, 0)
+
+        def query_step(step, inner):
+            target = member_at(step + 1)
+            rows = rows_of(target)
+            tiles = [None] * (group // LANES)
+            for head in range(heads):
+                first, last, start = head_span(head)
+                width = (last - first) * LANES
+                scores = lax.dot_general(
+                    q_h[head, rows, :width],
+                    k_h[head, :, :width],
+                    (((1,), (1,)), ((), ())),
+                    preferred_element_type=jnp.float32,
+                )
+                largest = jnp.max(scores, axis=-1, keepdims=True)
+                weights = jnp.exp2((scores - largest) * (HD ** (-0.5) * LOG2E))
+                mixed = jnp.dot(
+                    weights.astype(jnp.bfloat16),
+                    v_h[head, :, :width],
+                    preferred_element_type=jnp.float32,
+                )
+                spare = spare_lane(head)
+                mixed = mixed * (1.0 / mixed[:, spare : spare + 1])
+                for tile in range(first, last):
+                    piece = mixed[:, (tile - first) * LANES : (tile - first + 1) * LANES]
+                    if tiles[tile] is None:
+                        tiles[tile] = piece
+                    else:
+                        tiles[tile] = jnp.where(lane < head * HD - tile * LANES, tiles[tile], piece)
+            for tile, value in enumerate(tiles):
+                result[band, rows, tile * LANES : (tile + 1) * LANES] = value.astype(jnp.bfloat16)
+
+            @pl.when(step < members - 1)
+            def _():
+                homeward(band, step + 1).start()
+
+            @pl.when(step == members - 1)
+            def _():
+                stay(band).start()
+
+            return inner
+
+        lax.fori_loop(0, members, query_step, 0)
+        return carry
+
+    lax.fori_loop(0, bands, attend_band, 0)
+
+    weight_copy.wait()
+
+    def project(band, carry):
+        stay(band).wait()
+        for part in range(2):
+            token_copy(band, part).wait()
+        for distance in range(1, members):
+            homeward(band, distance).wait_recv()
+        for start in range(0, D, group):
+            columns = slice(start, start + group)
+            total = jnp.dot(
+                gathered[band], weight_v[:, columns], preferred_element_type=jnp.float32
+            )
+            total = total.reshape(WH, cols, group) + token_v[band, :, :, columns].astype(
+                jnp.float32
+            )
+            out_v[band, :, :, columns] = total.astype(jnp.bfloat16)
+        for part in range(2):
+            out_copy(band, part).start()
+        return carry
+
+    lax.fori_loop(0, bands, project, 0)
+
+    def drain(band, carry):
+        for part in range(2):
+            out_copy(band, part).wait()
+        for distance in range(1, members):
+            homeward(band, distance).wait_send()
+            for kind, part in pieces:
+                outgoing(band, distance, kind, part).wait_send()
+        return carry
+
+    lax.fori_loop(0, bands, drain, 0)
+
+
+def fused_device(qkv_grid, tokens, out_weight, regions):
+    windows = lax.axis_size("win")
+    members = lax.axis_size("seq")
+    lat, _, cols, packed = qkv_grid.shape
+    bands = lat // WH
+    group = D // members
+    heads = HEADS // members
+    block = WH * cols
+    window_tokens = WH * WW
+    labels = regions.reshape(lat, WW).astype(jnp.bfloat16)
+    behind = from_behind(labels, "win", 1)
+    labels = jnp.where(lax.axis_index("seq") < members // 2, behind, labels)
+    labels = labels.reshape(bands, WH, members, cols).transpose(0, 2, 1, 3)
+    labels = jnp.broadcast_to(
+        labels.reshape(bands, window_tokens, 1), (bands, window_tokens, LANES)
+    )
+    bf16 = jnp.bfloat16
+    wide = 2 * LANES
+    dma = pltpu.SemaphoreType.DMA
+    out = pl.pallas_call(
+        functools.partial(fused_kernel, windows, members, bands, cols),
+        out_shape=jax.ShapeDtypeStruct((lat, cols, D), bf16),
+        in_specs=[pl.BlockSpec(memory_space=pl.ANY)] * 4,
+        out_specs=pl.BlockSpec(memory_space=pl.ANY),
+        scratch_shapes=[
+            pltpu.VMEM((bands, 3, members, WH, cols, group), bf16),
+            pltpu.VMEM((bands, window_tokens, LANES), bf16),
+            pltpu.VMEM((D, D), bf16),
+            pltpu.VMEM((bands, WH, cols, D), bf16),
+            pltpu.VMEM((heads, window_tokens, wide), bf16),
+            pltpu.VMEM((heads, window_tokens, wide), bf16),
+            pltpu.VMEM((heads, window_tokens, wide), bf16),
+            pltpu.VMEM((bands, window_tokens, group), bf16),
+            pltpu.VMEM((bands, block, D), bf16),
+            pltpu.VMEM((bands, WH, cols, D), bf16),
+            dma((bands, members - 1, 3, 2)),
+            dma((bands, members - 1, 3, 2)),
+            dma((bands, 3, 2)),
+            dma((bands, members - 1)),
+            dma((bands, members - 1)),
+            dma((bands,)),
+            dma((bands, 2)),
+            dma((bands, 2)),
+            dma((2,)),
+        ],
+        compiler_params=pltpu.CompilerParams(
+            collective_id=0, has_side_effects=True, vmem_limit_bytes=56 * 1024 * 1024
+        ),
+    )(
+        qkv_grid.reshape(lat, cols, packed),
+        tokens.reshape(lat, cols, D),
+        out_weight,
+        labels,
+    )
+    return out.reshape(tokens.shape)
+
+
+def per_device(qkv_grid, tokens, out_weight, regions):
+    members = lax.axis_size("seq")
+    group = D // members
+    fits = members % 2 == 0 and group % LANES == 0 and qkv_grid.shape[2] % ROWS8 == 0
+    if fits:
+        return fused_device(qkv_grid, tokens, out_weight, regions)
+    return general_device(qkv_grid, tokens, out_weight, regions)
+
+
 def solution(mesh):
     in_specs = (P(None, "win", "seq", None), P(None, "win", "seq", None), P(), P(None, "win", None))
     out_specs = P(None, "win", "seq", None)

time: 491 us -> 209 us (0.43)
  blocking collectives: 264 us -> 0 us
  Pallas kernels: 0 us -> 198 us
  local copies, waits for them, and re-layouts: 80.1 us -> 4.84 us
  waiting for transfers between devices: 67.3 us -> 3.97 us
  matrix products: 60.3 us -> 0 us
  other arithmetic: 13.8 us -> 1.44 us
    all_to_all x2 -> x0, blocking collectives: 264 us -> none  [the longest x1 196 us: per_device(): lax.all_to_all(split_heads, 'seq', split_axis=4, concat_axis=2, tiled=True)]
    pallas_call x0 -> x1, Pallas kernels: none -> 198 us  [fused_device(): pl.pallas_call(functools.partial(fused_kernel, windows, members, bands, c...]
    ppermute x2 -> x1, waiting for transfers between devices: 67.3 us -> 3.97 us  [from_behind(): return lax.ppermute(block, axis, route)]
    dot_general x4 -> x0, matrix products: 31.9 us -> none  [the longest x3 23.3 us: attend(): jnp.einsum('hqk,khd->qhd', soft_weights, values, preferred_element_type=j...]
    sub x3 -> x0, matrix products: 28.4 us -> none  [attend(): weights = jnp.exp(scores - largest)]
    reshape x3 -> x1, local copies, waits for them, and re-layouts: 24.8 us -> 0.08 us  [fused_device(): labels = labels.reshape(bands, WH, members, cols).transpose(0, 2, 1, 3)]
    while x2 -> x0, local copies, waits for them, and re-layouts: 14.6 us -> none  [window_attention(): attended = lax.map(one_window, (blocks, labels))]
    concatenate x3 -> x0, other arithmetic: 11.4 us -> none  [the longest x1 5.96 us: per_device(): shifted = jnp.roll(shifted, -half_rows, axis=0)]
  transfers between devices with their start and end apart: 2 -> 1, of which waited for: 2 -> 1; matrix products, arithmetic and copies ran while one was open for 0% -> 0% of each run, Pallas kernels for 0% -> 0%
where the time goes in v1:
time: 209 us; the launch traced here: 208 us
  Pallas kernels  198 us (95%)
  local copies, waits for them, and re-layouts  4.84 us (2%)
  waiting for transfers between devices  3.97 us (2%)
    pallas_call x1, Pallas kernels, fused_device(): pl.pallas_call(functools.partial(fused_kernel, windows, members, bands, c...  198 us
  transfers between devices with their start and end apart: 1, of which 1 were waited for; matrix products, arithmetic and copies ran while one was open for 0% of the time, Pallas kernels for 0%

profile of v1, /device:TPU:8, one launch (start us, length us, event | category | flops | bytes accessed | tf_op | source)
XLA Modules:
  0.0 208.2 jit_solution(16112126119311574163)
XLA Ops:
  0.0 0.7 convert_bitcast_fusion
  0.7 0.0 collective-permute-start
  0.7 4.0 %collective-permute-done = bf16[90,32]{0,1:T(8,128)(2,1)S(1)} collective-permute-done((bf16[90,32]{0,1:T(8,128)(2,1)S(1)}, bf16[90,32]{0,1:T(8,128)(2,1)S(1)}, u32[]{:S(2)}, u32[]{:S(2)}) %collective-permute-start) | collective-permute-done | bytes 5792 | tf_op jit(solution)/shard_map/ppermute | solution.py:20
  4.7 0.7 broadcast_select_fusion
  5.4 0.1 reshape.18
  5.5 0.2 copy.7
  5.7 0.1 broadcast_in_dim.7
  5.8 1.3 broadcast_in_dim.8.label_ref
  7.1 197.9 %shard_map.46 = bf16[90,8,1536]{2,1,0:T(8,128)(2,1)} custom-call(bf16[90,8,4608]{2,1,0:T(8,128)(2,1)} %bitcast.13, bf16[90,8,1536]{2,1,0:T(8,128)(2,1)} %bitcast.14, bf16[1536,1536]{1,0:T(8,128)(2,1)} %weight_ref.1, bf16[3,960,128]{2,1,0:T(8,128)(2,1)} %broadcast_in_dim.8.label_ref), custom_call_target="tpu_custom_call" | custom-call | tf_op jit(solution)/shard_map/pallas_call | solution.py:379
  205.0 3.1 %copy.10 = bf16[90,1,8,1536]{3,2,1,0:T(8,128)(2,1)} copy(bf16[90,1,8,1536]{3,2,1,0:T(8,128)(2,1)} %bitcast.12) | data formatting | bytes 4423680
Async XLA Ops:
  0.7 4.0 %collective-permute-start = (bf16[90,32]{0,1:T(8,128)(2,1)S(1)}, bf16[90,32]{0,1:T(8,128)(2,1)S(1)}, u32[]{:S(2)}, u32[]{:S(2)}) collective-permute-start(bf16[90,32]{0,1:T(8,128)(2,1)S(1)} %convert_bitcast_fusion), channel_id=1, source_target_pairs={{28,0},{0,4},{4,8},{8,12},{12,16},{16,20},{20,24},{24,28},{29,1},{... | collective-permute-start | bytes 17288 | tf_op jit(solution)/shard_map/ppermute | solution.py:20

commit v2 on v1

--- a/solution.py
+++ b/solution.py
@@ -122,7 +122,7 @@
     v_h,
     result,
     gathered,
-    out_v,
+    total_v,
     send_sem,
     recv_sem,
     own_sem,
@@ -130,8 +130,8 @@
     back_recv,
     back_own,
     token_sem,
-    out_sem,
-    misc_sem,
+    label_sem,
+    weight_sem,
 ):
     half_rows = WH // 2
     half_n = members // 2
@@ -184,13 +184,6 @@
             token_sem.at[band, part],
         )
 
-    def out_copy(band, part):
-        return pltpu.make_async_copy(
-            out_v.at[band, pl.ds(part * half_rows, half_rows)],
-            out_ref.at[pl.ds(grid_row(band, part), half_rows)],
-            out_sem.at[band, part],
-        )
-
     def rows_of(member):
         return pl.ds(pl.multiple_of(member * block, block), block)
 
@@ -212,8 +205,16 @@
             back_own.at[band],
         )
 
-    label_copy = pltpu.make_async_copy(label_ref, label_v, misc_sem.at[0])
-    weight_copy = pltpu.make_async_copy(weight_ref, weight_v, misc_sem.at[1])
+    own_labels = pltpu.make_async_copy(label_ref, label_v, label_sem.at[2])
+    sent_labels = pltpu.make_async_remote_copy(
+        src_ref=label_ref,
+        dst_ref=label_v,
+        send_sem=label_sem.at[0],
+        recv_sem=label_sem.at[1],
+        device_id=device_of(member_at(half_n)),
+        device_id_type=pl.DeviceIdType.MESH,
+    )
+    weight_copy = pltpu.make_async_copy(weight_ref, weight_v, weight_sem)
 
     barrier = pltpu.get_barrier_semaphore()
     for distance in range(1, members):
@@ -235,20 +236,40 @@
             own(band, kind, part).start()
         return carry
 
+    @pl.when(low == 0)
+    def _():
+        sent_labels.start()
+        own_labels.start()
+
     lax.fori_loop(0, bands, launch, 0)
-    label_copy.start()
     weight_copy.start()
     for band in range(bands):
         for part in range(2):
             token_copy(band, part).start()
-    label_copy.wait()
+
+    @pl.when(low == 0)
+    def _():
+        own_labels.wait()
+
+    @pl.when(low == 1)
+    def _():
+        sent_labels.wait_recv()
 
     lane = lax.broadcasted_iota(jnp.int32, (block, LANES), 1)
     slot = lax.rem(lane, 32).astype(jnp.float32)
+    spread = (WH, cols, WW)
+    column_id = lax.broadcasted_iota(jnp.int32, spread, 2)
+    cell_id = lax.broadcasted_iota(jnp.int32, spread, 1)
 
     def prepare(band, member):
         rows = rows_of(member)
-        label = label_v[band, rows, :].astype(jnp.float32)
+        band_labels = label_v[pl.ds(band * WH, WH)].astype(jnp.float32)
+        picked = jnp.where(
+            column_id == cell_id + member * cols, jnp.broadcast_to(band_labels, spread), 0.0
+        )
+        label = jnp.broadcast_to(
+            jnp.sum(picked, axis=-1, keepdims=True), (WH, cols, LANES)
+        ).reshape(block, LANES)
         same = slot == label
         query_fill = jnp.where(same, FAR, 0.0)
         key_fill = jnp.where(same, 0.0, jnp.where(slot < REGION_SLOTS, 1.0, 0.0))
@@ -324,30 +345,45 @@
 
     weight_copy.wait()
 
+    def partial_of(band, member, columns):
+        return jnp.dot(
+            gathered[band, :, features(0, member)],
+            weight_v[features(0, member), columns],
+            preferred_element_type=jnp.float32,
+        )
+
     def project(band, carry):
         stay(band).wait()
         for part in range(2):
             token_copy(band, part).wait()
-        for distance in range(1, members):
-            homeward(band, distance).wait_recv()
-        for start in range(0, D, group):
-            columns = slice(start, start + group)
-            total = jnp.dot(
-                gathered[band], weight_v[:, columns], preferred_element_type=jnp.float32
-            )
-            total = total.reshape(WH, cols, group) + token_v[band, :, :, columns].astype(
-                jnp.float32
-            )
-            out_v[band, :, :, columns] = total.astype(jnp.bfloat16)
-        for part in range(2):
-            out_copy(band, part).start()
+        for distance in range(members):
+            if distance > 0:
+                homeward(band, distance).wait_recv()
+            source = member_at(members - distance)
+            for start in range(0, D, group):
+                columns = slice(start, start + group)
+                term = partial_of(band, source, columns)
+                if distance == 0:
+                    total_v[:, columns] = term
+                elif distance < members - 1:
+                    total_v[:, columns] += term
+                else:
+                    total = (total_v[:, columns] + term).reshape(WH, cols, group)
+                    total = total + token_v[band, :, :, columns].astype(jnp.float32)
+                    total = total.astype(jnp.bfloat16)
+                    for part in range(2):
+                        out_ref[pl.ds(grid_row(band, part), half_rows), :, columns] = total[
+                            part * half_rows : (part + 1) * half_rows
+                        ]
         return carry
 
     lax.fori_loop(0, bands, project, 0)
 
+    @pl.when(low == 0)
+    def _():
+        sent_labels.wait_send()
+
     def drain(band, carry):
-        for part in range(2):
-            out_copy(band, part).wait()
         for distance in range(1, members):
             homeward(band, distance).wait_send()
             for kind, part in pieces:
@@ -366,24 +402,17 @@
     heads = HEADS // members
     block = WH * cols
     window_tokens = WH * WW
-    labels = regions.reshape(lat, WW).astype(jnp.bfloat16)
-    behind = from_behind(labels, "win", 1)
-    labels = jnp.where(lax.axis_index("seq") < members // 2, behind, labels)
-    labels = labels.reshape(bands, WH, members, cols).transpose(0, 2, 1, 3)
-    labels = jnp.broadcast_to(
-        labels.reshape(bands, window_tokens, 1), (bands, window_tokens, LANES)
-    )
     bf16 = jnp.bfloat16
     wide = 2 * LANES
     dma = pltpu.SemaphoreType.DMA
     out = pl.pallas_call(
         functools.partial(fused_kernel, windows, members, bands, cols),
-        out_shape=jax.ShapeDtypeStruct((lat, cols, D), bf16),
+        out_shape=pltpu.VMEM((lat, cols, D), bf16),
         in_specs=[pl.BlockSpec(memory_space=pl.ANY)] * 4,
-        out_specs=pl.BlockSpec(memory_space=pl.ANY),
+        out_specs=pl.BlockSpec(memory_space=pltpu.VMEM),
         scratch_shapes=[
             pltpu.VMEM((bands, 3, members, WH, cols, group), bf16),
-            pltpu.VMEM((bands, window_tokens, LANES), bf16),
+            pltpu.VMEM((lat, 1, WW), jnp.int32),
             pltpu.VMEM((D, D), bf16),
             pltpu.VMEM((bands, WH, cols, D), bf16),
             pltpu.VMEM((heads, window_tokens, wide), bf16),
@@ -391,7 +420,7 @@
             pltpu.VMEM((heads, window_tokens, wide), bf16),
             pltpu.VMEM((bands, window_tokens, group), bf16),
             pltpu.VMEM((bands, block, D), bf16),
-            pltpu.VMEM((bands, WH, cols, D), bf16),
+            pltpu.VMEM((block, D), jnp.float32),
             dma((bands, members - 1, 3, 2)),
             dma((bands, members - 1, 3, 2)),
             dma((bands, 3, 2)),
@@ -399,8 +428,8 @@
             dma((bands, members - 1)),
             dma((bands,)),
             dma((bands, 2)),
-            dma((bands, 2)),
-            dma((2,)),
+            dma((3,)),
+            dma,
         ],
         compiler_params=pltpu.CompilerParams(
             collective_id=0, has_side_effects=True, vmem_limit_bytes=56 * 1024 * 1024
@@ -409,7 +438,7 @@
         qkv_grid.reshape(lat, cols, packed),
         tokens.reshape(lat, cols, D),
         out_weight,
-        labels,
+        regions,
     )
     return out.reshape(tokens.shape)
 

time: 209 us -> 202 us (0.967)
  waiting for transfers between devices: 3.97 us -> 0 us
    ppermute x1 -> x0, waiting for transfers between devices: 3.97 us -> none  [from_behind(): return lax.ppermute(block, axis, route)]
  transfers between devices with their start and end apart: 1 -> 0, of which waited for: 1 -> 0; matrix products, arithmetic and copies ran while one was open for 0% -> 0% of each run, Pallas kernels for 0% -> 0%
where the time goes in v2:
time: 202 us
  Pallas kernels  199 us (99%)
  local copies, waits for them, and re-layouts  2.79 us (1%)
    pallas_call x1, Pallas kernels, fused_device(): pl.pallas_call(functools.partial(fused_kernel, windows, members, bands, c...  199 us

profile of v2, /device:TPU:8, one launch (start us, length us, event | category | flops | bytes accessed | tf_op | source)
XLA Modules:
  0.0 202.1 jit_solution(765151170194928043)
XLA Ops:
  0.0 1.4 copy.5.label_ref
  1.4 199.3 %shard_map.46 = bf16[90,8,1536]{2,1,0:T(8,128)(2,1)S(1)} custom-call(bf16[90,8,4608]{2,1,0:T(8,128)(2,1)} %bitcast.6, bf16[90,8,1536]{2,1,0:T(8,128)(2,1)} %bitcast.7, bf16[1536,1536]{1,0:T(8,128)(2,1)} %weight_ref.1, s32[90,1,32]{2,1,0:T(1,128)} %copy.5.label_ref), custom_call_target="tpu_custom_call" | custom-call | tf_op jit(solution)/shard_map/pallas_call | solution.py:408
  200.7 1.4 copy.8

commit v3 on v2

--- a/solution.py
+++ b/solution.py
@@ -257,15 +257,16 @@
 
     lane = lax.broadcasted_iota(jnp.int32, (block, LANES), 1)
     slot = lax.rem(lane, 32).astype(jnp.float32)
-    spread = (WH, cols, WW)
-    column_id = lax.broadcasted_iota(jnp.int32, spread, 2)
-    cell_id = lax.broadcasted_iota(jnp.int32, spread, 1)
+    spread = (WH, cols, lat)
+    row_lane = lax.broadcasted_iota(jnp.int32, spread, 2)
+    row_id = lax.broadcasted_iota(jnp.int32, spread, 0)
 
     def prepare(band, member):
         rows = rows_of(member)
-        band_labels = label_v[pl.ds(band * WH, WH)].astype(jnp.float32)
+        seats = pl.ds(pl.multiple_of(member * cols, cols), cols)
+        member_labels = label_v[:, seats, :].astype(jnp.float32)
         picked = jnp.where(
-            column_id == cell_id + member * cols, jnp.broadcast_to(band_labels, spread), 0.0
+            row_lane == row_id + band * WH, jnp.broadcast_to(member_labels, spread), 0.0
         )
         label = jnp.broadcast_to(
             jnp.sum(picked, axis=-1, keepdims=True), (WH, cols, LANES)
@@ -412,7 +413,7 @@
         out_specs=pl.BlockSpec(memory_space=pltpu.VMEM),
         scratch_shapes=[
             pltpu.VMEM((bands, 3, members, WH, cols, group), bf16),
-            pltpu.VMEM((lat, 1, WW), jnp.int32),
+            pltpu.VMEM((1, WW, lat), jnp.int32),
             pltpu.VMEM((D, D), bf16),
             pltpu.VMEM((bands, WH, cols, D), bf16),
             pltpu.VMEM((heads, window_tokens, wide), bf16),
@@ -438,7 +439,7 @@
         qkv_grid.reshape(lat, cols, packed),
         tokens.reshape(lat, cols, D),
         out_weight,
-        regions,
+        regions.transpose(1, 2, 0),
     )
     return out.reshape(tokens.shape)
 

time: 202 us -> 200 us (0.990)
  no operation moved by 1% of the time
where the time goes in v3:
time: 200 us; the launch traced here: 199 us
  Pallas kernels  198 us (99%)
    pallas_call x1, Pallas kernels, fused_device(): pl.pallas_call(functools.partial(fused_kernel, windows, members, bands, c...  198 us

profile of v3, /device:TPU:8, one launch (start us, length us, event | category | flops | bytes accessed | tf_op | source)
XLA Modules:
  0.0 199.4 jit_solution(4053899353943331682)
XLA Ops:
  0.0 198.0 %shard_map.46 = bf16[90,8,1536]{2,1,0:T(8,128)(2,1)S(1)} custom-call(bf16[90,8,4608]{2,1,0:T(8,128)(2,1)} %bitcast.7, bf16[90,8,1536]{2,1,0:T(8,128)(2,1)} %bitcast.8, bf16[1536,1536]{1,0:T(8,128)(2,1)} %weight_ref.1, s32[1,32,90]{2,1,0:T(8,128)} %bitcast.9), custom_call_target="tpu_custom_call" | custom-call | tf_op jit(solution)/shard_map/pallas_call | solution.py:409
  198.0 1.4 copy.7

commit v4 on v3

--- a/solution.py
+++ b/solution.py
@@ -229,8 +229,8 @@
     pieces = [(kind, part) for kind in range(3) for part in range(2)]
 
     def launch(band, carry):
-        for kind, part in pieces:
-            for distance in range(1, members):
+        for distance in [*range(members // 2, members), *range(1, members // 2)]:
+            for kind, part in pieces:
                 outgoing(band, distance, kind, part).start()
         for kind, part in pieces:
             own(band, kind, part).start()

time: 200 us -> 199 us (level)
  no operation moved by 1% of the time
where the time goes in v4:
time: 199 us
  Pallas kernels  198 us (99%)
    pallas_call x1, Pallas kernels, fused_device(): pl.pallas_call(functools.partial(fused_kernel, windows, members, bands, c...  198 us

profile of v4, /device:TPU:8, one launch (start us, length us, event | category | flops | bytes accessed | tf_op | source)
XLA Modules:
  0.0 199.3 jit_solution(2602788720546995146)
XLA Ops:
  0.0 197.9 %shard_map.46 = bf16[90,8,1536]{2,1,0:T(8,128)(2,1)S(1)} custom-call(bf16[90,8,4608]{2,1,0:T(8,128)(2,1)} %bitcast.7, bf16[90,8,1536]{2,1,0:T(8,128)(2,1)} %bitcast.8, bf16[1536,1536]{1,0:T(8,128)(2,1)} %weight_ref.1, s32[1,32,90]{2,1,0:T(8,128)} %bitcast.9), custom_call_target="tpu_custom_call" | custom-call | tf_op jit(solution)/shard_map/pallas_call | solution.py:409
  198.0 1.4 copy.7
